TPU v7x, 32 devices: a whole 2x2x4 slice. The times are simulated.
32 devices in a mesh: shard: 4 (over z), ctx: 2 (over x), tp: 4 (over y, core).
Axes of the slice: x: 2, y: 2, z: 4, core: 2. Of those that a mesh axis runs over, the one named last changes fastest.
Arguments:
- tokens: bfloat16 [4, 1024, 768], P('shard', 'ctx'), may hold values from -6 to 6
- segment_ids: int32 [4, 1024], P('shard', 'ctx'), may hold values from 0 to 15, never falling along the last dimension, each value on 1 to 512 neighbouring positions
- valid_mask: int32 [4, 1024], P('shard', 'ctx'), may hold values from 0 to 1, as said below
- qkv_weight: bfloat16 [3, 768, 768], P(None, ('shard', 'ctx'), 'tp'), may hold values from -0.21875 to 0.21875
- qv_bias: float32 [2, 768], P(None, 'tp'), may hold values from -0.4375 to 0.4375
- out_weight: bfloat16 [768, 768], P('tp', ('shard', 'ctx')), may hold values from -2.5 to 2.5
- out_bias: float32 [768], replicated, may hold values from -1.5 to 1.5
- norm1_gain: float32 [768], replicated, may hold values from 0.5 to 1.5
- norm1_shift: float32 [768], replicated, may hold values from -1.5 to 1.5
- in_weight: bfloat16 [768, 3072], P(('shard', 'ctx'), 'tp'), may hold values from -0.21875 to 0.21875
- in_bias: float32 [3072], P('tp'), may hold values from -4 to 4
- down_weight: bfloat16 [3072, 768], P('tp', ('shard', 'ctx')), may hold values from -0.109375 to 0.109375
- down_bias: float32 [768], replicated, may hold values from -1.5 to 1.5
- norm2_gain: float32 [768], replicated, may hold values from 0.5 to 1.5
- norm2_shift: float32 [768], replicated, may hold values from -1.5 to 1.5
- out_cotangent: float32 [4, 1024, 768], P('shard', 'ctx'), may hold values from -6 to 6
Outputs:
- layer_out: bfloat16 [4, 1024, 768], P('shard', 'ctx')
- tokens_grad: float32 [4, 1024, 768], P('shard', 'ctx')
- qkv_weight_grad: float32 [3, 768, 768], P(None, ('shard', 'ctx'), 'tp')
- qv_bias_grad: float32 [2, 768], P(None, 'tp')
- out_weight_grad: float32 [768, 768], P('tp', ('shard', 'ctx'))
- out_bias_grad: float32 [768], replicated
- norm1_gain_grad: float32 [768], replicated
- norm1_shift_grad: float32 [768], replicated
- in_weight_grad: float32 [768, 3072], P(('shard', 'ctx'), 'tp')
- in_bias_grad: float32 [3072], P('tp')
- down_weight_grad: float32 [3072, 768], P('tp', ('shard', 'ctx'))
- down_bias_grad: float32 [768], replicated
- norm2_gain_grad: float32 [768], replicated
- norm2_shift_grad: float32 [768], replicated
- stream_rms: float32 [3], replicated
Inputs may be any that keep to these rules, and one draw needn't show every extreme that they name: `segment_ids`: in each sequence the document numbers never fall; each of the 16 documents holds 1 to 512 tokens, and one holds exactly 512. In each sequence the tokens with valid_mask 1 are a leading run of 512 to 1024 positions.
All inputs are finite; a program needn't handle non-finite values.
Results may differ from a plain program's by a relative error of at most 0.012.
Values may be sent and summed in bfloat16 or wider, within the bound.
A program may use at most 128 MiB of HBM per device.

v0:
```python
import jax
import jax.numpy as jnp
from jax import lax
from jax.sharding import PartitionSpec as P

HEAD_DIM = 64
norm_eps = 1e-12
masked_score = -1e30


def layer_norm(rows, gain, shift):
    mean = jnp.mean(rows, axis=-1, keepdims=True)
    centred = rows - mean
    spread = jnp.mean(centred * centred, axis=-1, keepdims=True)
    return centred * lax.rsqrt(spread + norm_eps) * gain + shift


def gelu_tanh(value):
    return jax.nn.gelu(value, approximate=True)


def allowed_pairs(query_seg, query_pos, key_seg, key_valid, key_pos):
    same = query_seg[:, None] == key_seg[None, :]
    usable = (key_valid[None, :] == 1) | (query_pos[:, None] == key_pos[None, :])
    return same & usable


def scaled_scores(left, right):
    return jnp.einsum("ae,be->ab", left, right, preferred_element_type=jnp.float32) * 0.125


def softmax_parts(scores, mask):
    masked = jnp.where(mask, scores, masked_score)
    top = jnp.max(masked, axis=1)
    weights = jnp.where(mask, jnp.exp(masked - top[:, None]), 0.0)
    return (top, jnp.sum(weights, axis=1), weights)


def rebuilt_probs(scores, mask, top, total):
    masked = jnp.where(mask, scores, masked_score)
    weights = jnp.where(mask, jnp.exp(masked - top[:, None]), 0.0)
    return weights / total[:, None]


def body(
    tokens,
    segment_ids,
    valid_mask,
    qkv_weight,
    qv_bias,
    out_weight,
    out_bias,
    norm1_gain,
    norm1_shift,
    in_weight,
    in_bias,
    down_weight,
    down_bias,
    norm2_gain,
    norm2_shift,
    out_cotangent,
):
    seqs_here, piece, width = tokens.shape
    rows = seqs_here * piece
    cols = qkv_weight.shape[2]
    heads_here = cols // HEAD_DIM
    w_qkv, w_out, w_in, w_down = (
        lax.all_gather(qkv_weight, ("shard", "ctx"), axis=1, tiled=True),
        lax.all_gather(out_weight, ("shard", "ctx"), axis=1, tiled=True),
        lax.all_gather(in_weight, ("shard", "ctx"), axis=0, tiled=True),
        lax.all_gather(down_weight, ("shard", "ctx"), axis=1, tiled=True),
    )
    flat = tokens.reshape(rows, width)
    projected = jnp.einsum("nd,jdc->jnc", flat, w_qkv, preferred_element_type=jnp.float32)
    queries = (projected[0] + qv_bias[0]).astype(jnp.bfloat16).reshape(seqs_here, piece, cols)
    keys = projected[1].astype(jnp.bfloat16).reshape(seqs_here, piece, cols)
    values = (projected[2] + qv_bias[1]).astype(jnp.bfloat16).reshape(seqs_here, piece, cols)
    marks = lax.all_gather(jnp.stack([segment_ids, valid_mask]), "ctx", axis=2, tiled=True)
    kv_all = lax.all_gather(jnp.stack([keys, values]), "ctx", axis=2, tiled=True)
    seq_len = kv_all.shape[2]
    own_pos = lax.axis_index("ctx") * piece + lax.iota(jnp.int32, piece)
    all_pos = lax.iota(jnp.int32, seq_len)
    seq = 0
    mask = allowed_pairs(segment_ids[seq], own_pos, marks[0, seq], marks[1, seq], all_pos)
    masks = [mask]
    head_tops = []
    head_totals = []
    head_out = []
    for head in range(heads_here):
        span = slice(head * HEAD_DIM, (head + 1) * HEAD_DIM)
        scores = scaled_scores(queries[seq, :, span], kv_all[0, seq, :, span])
        top, total, weights = softmax_parts(scores, mask)
        probs = (weights / total[:, None]).astype(jnp.bfloat16)
        head_out.append(jnp.dot(probs, kv_all[1, seq, :, span], preferred_element_type=jnp.float32))
        head_tops.append(top)
        head_totals.append(total)
    context_parts = [jnp.concatenate(head_out, axis=1)]
    seq_tops = [jnp.stack(head_tops)]
    seq_totals = [jnp.stack(head_totals)]
    context = jnp.stack(context_parts).reshape(rows, cols).astype(jnp.bfloat16)
    top_all = jnp.stack(seq_tops)
    total_all = jnp.stack(seq_totals)
    attn = lax.psum(jnp.dot(context, w_out, preferred_element_type=jnp.float32), "tp") + out_bias
    hidden, norm1_back = jax.vjp(
        layer_norm, flat.astype(jnp.float32) + attn, norm1_gain, norm1_shift
    )
    hidden_low = hidden.astype(jnp.bfloat16)
    pre = jnp.dot(hidden_low, w_in, preferred_element_type=jnp.float32) + in_bias
    act, gelu_back = jax.vjp(gelu_tanh, pre)
    act_low = act.astype(jnp.bfloat16)
    ffn = lax.psum(jnp.dot(act_low, w_down, preferred_element_type=jnp.float32), "tp") + down_bias
    out_rows, norm2_back = jax.vjp(layer_norm, hidden + ffn, norm2_gain, norm2_shift)
    layer_out = out_rows.astype(jnp.bfloat16).reshape(seqs_here, piece, width)
    w_qkv, w_out, w_in, w_down = (
        lax.all_gather(qkv_weight, ("shard", "ctx"), axis=1, tiled=True),
        lax.all_gather(out_weight, ("shard", "ctx"), axis=1, tiled=True),
        lax.all_gather(in_weight, ("shard", "ctx"), axis=0, tiled=True),
        lax.all_gather(down_weight, ("shard", "ctx"), axis=1, tiled=True),
    )
    d_resid2, d_gain2, d_shift2 = norm2_back(out_cotangent.reshape(rows, width))
    d_ffn = d_resid2.astype(jnp.bfloat16)
    d_down_bias = jnp.sum(d_ffn.astype(jnp.float32), axis=0)
    g_down = jnp.einsum("nf,nd->fd", act_low, d_ffn, preferred_element_type=jnp.float32)
    d_act = jnp.einsum("nd,fd->nf", d_ffn, w_down, preferred_element_type=jnp.float32)
    d_pre = gelu_back(d_act)[0].astype(jnp.bfloat16)
    d_in_bias = jnp.sum(d_pre.astype(jnp.float32), axis=0)
    g_in = jnp.einsum("nd,nf->df", hidden_low, d_pre, preferred_element_type=jnp.float32)
    d_hidden = d_resid2 + lax.psum(
        jnp.einsum("nf,df->nd", d_pre, w_in, preferred_element_type=jnp.float32), "tp"
    )
    d_resid1, d_gain1, d_shift1 = norm1_back(d_hidden)
    d_attn = d_resid1.astype(jnp.bfloat16)
    d_out_bias = jnp.sum(d_attn.astype(jnp.float32), axis=0)
    g_out = jnp.einsum("nc,nd->cd", context, d_attn, preferred_element_type=jnp.float32)
    d_context = (
        jnp.einsum("nd,cd->nc", d_attn, w_out, preferred_element_type=jnp.float32)
        .astype(jnp.bfloat16)
        .reshape(seqs_here, piece, cols)
    )
    delta_parts = []
    seq = 0
    dq_heads = []
    dk_heads = []
    dv_heads = []
    delta_heads = []
    for head in range(heads_here):
        span = slice(head * HEAD_DIM, (head + 1) * HEAD_DIM)
        q_head = queries[seq, :, span]
        k_every = kv_all[0, seq, :, span]
        d_head = d_context[seq, :, span]
        probs = rebuilt_probs(
            scaled_scores(q_head, k_every), masks[seq], top_all[seq, head], total_all[seq, head]
        )
        d_probs = jnp.einsum(
            "qe,ke->qk", d_head, kv_all[1, seq, :, span], preferred_element_type=jnp.float32
        )
        delta = jnp.sum(probs * d_probs, axis=1)
        d_scores = (probs * (d_probs - delta[:, None])).astype(jnp.bfloat16)
        dq_heads.append(jnp.dot(d_scores, k_every, preferred_element_type=jnp.float32) * 0.125)
        delta_heads.append(delta)
        dk_heads.append(
            jnp.einsum("qk,qe->ke", d_scores, q_head, preferred_element_type=jnp.float32) * 0.125
        )
        dv_heads.append(
            jnp.einsum(
                "qk,qe->ke", probs.astype(jnp.bfloat16), d_head, preferred_element_type=jnp.float32
            )
        )
    query_parts = [jnp.concatenate(dq_heads, axis=1)]
    delta_parts.append(jnp.stack(delta_heads))
    key_parts = [jnp.concatenate(dk_heads, axis=1)]
    value_parts = [jnp.concatenate(dv_heads, axis=1)]
    d_queries = jnp.stack(query_parts).reshape(rows, cols).astype(jnp.bfloat16)
    key_sums, value_sums = (
        lax.psum_scatter(jnp.stack(key_parts), "ctx", scatter_dimension=1, tiled=True),
        lax.psum_scatter(jnp.stack(value_parts), "ctx", scatter_dimension=1, tiled=True),
    )
    d_keys = key_sums.reshape(rows, cols).astype(jnp.bfloat16)
    d_values = value_sums.reshape(rows, cols).astype(jnp.bfloat16)
    d_proj = jnp.stack([d_queries, d_keys, d_values])
    g_qkv = jnp.einsum("nd,jnc->jdc", flat, d_proj, preferred_element_type=jnp.float32)
    d_qv_bias = jnp.stack(
        [
            jnp.sum(d_queries.astype(jnp.float32), axis=0),
            jnp.sum(d_values.astype(jnp.float32), axis=0),
        ]
    )
    d_flat = d_resid1 + lax.psum(
        jnp.einsum("jnc,jdc->nd", d_proj, w_qkv, preferred_element_type=jnp.float32), "tp"
    )
    tokens_grad = d_flat.reshape(seqs_here, piece, width)
    g_qkv_own, g_out_own, g_in_own, g_down_own = (
        lax.psum_scatter(g_qkv, ("shard", "ctx"), scatter_dimension=1, tiled=True),
        lax.psum_scatter(g_out, ("shard", "ctx"), scatter_dimension=1, tiled=True),
        lax.psum_scatter(g_in, ("shard", "ctx"), scatter_dimension=0, tiled=True),
        lax.psum_scatter(g_down, ("shard", "ctx"), scatter_dimension=1, tiled=True),
    )
    valid_rows = valid_mask.reshape(rows, 1).astype(jnp.float32)
    x_rows = flat.astype(jnp.float32)
    stats = jnp.stack(
        [
            jnp.sum(valid_rows * x_rows * x_rows),
            jnp.sum(valid_rows * attn * attn),
            jnp.sum(valid_rows * ffn * ffn),
            jnp.sum(valid_rows),
        ]
    )
    summed = lax.psum(
        (
            d_qv_bias,
            d_out_bias,
            d_gain1,
            d_shift1,
            d_in_bias,
            d_down_bias,
            d_gain2,
            d_shift2,
            stats,
        ),
        ("shard", "ctx"),
    )
    totals = summed[8]
    stream_rms = jnp.sqrt(totals[:3] / (totals[3] * width))
    return (
        layer_out,
        tokens_grad,
        g_qkv_own,
        summed[0],
        g_out_own,
        summed[1],
        summed[2],
        summed[3],
        g_in_own,
        summed[4],
        g_down_own,
        summed[5],
        summed[6],
        summed[7],
        stream_rms,
    )


def solution(mesh):
    return jax.shard_map(
        body,
        mesh=mesh,
        in_specs=(
            P("shard", "ctx", None),
            P("shard", "ctx"),
            P("shard", "ctx"),
            P(None, ("shard", "ctx"), "tp"),
            P(None, "tp"),
            P("tp", ("shard", "ctx")),
            P(),
            P(),
            P(),
            P(("shard", "ctx"), "tp"),
            P("tp"),
            P("tp", ("shard", "ctx")),
            P(),
            P(),
            P(),
            P("shard", "ctx", None),
        ),
        out_specs=(
            P("shard", "ctx", None),
            P("shard", "ctx", None),
            P(None, ("shard", "ctx"), "tp"),
            P(None, "tp"),
            P("tp", ("shard", "ctx")),
            P(),
            P(),
            P(),
            P(("shard", "ctx"), "tp"),
            P("tp"),
            P("tp", ("shard", "ctx")),
            P(),
            P(),
            P(),
            P(),
        ),
        check_vma=False,
    )
```

profile of v0, /device:TPU:0, one launch (start us, length us, event | category | flops | bytes accessed | tf_op | source)
XLA Modules:
  0.0 687.0 jit_solution(15073184442933198201)
XLA Ops:
  8.8 5.2 all_gather.22
  15.9 38.3 %all_gather.23 = bf16[3,768,192]{2,0,1:T(4,128)(2,1)S(1)} all-gather(bf16[3,96,192]{2,0,1:T(4,128)(2,1)S(1)} %copy.34), channel_id=1, replica_groups=mesh['shard'=4,'ctx'=2,'tp'=4] {'shard','ctx'}, dimensions={1}, use_global_device_ids=true | all-gather | bytes 995328 | tf_op jit(solution)/shard_map/all_gather | solution.py:68
  55.7 8.5 %all_gather.24 = bf16[2,1,1024,192]{2,3,1,0:T(8,128)(2,1)S(1)} all-gather(bf16[2,1,512,192]{2,3,1,0:T(8,128)(2,1)S(1)} %pad_maximum_fusion.1), channel_id=1, replica_groups=mesh['shard'=4,'ctx'=2,'tp'=4] {'ctx'}, dimensions={2}, use_global_device_ids=true | all-gather | bytes 1179648 | tf_op jit(solution)/shard_map/all_gather | solution.py:79
  64.2 2.2 fusion.65
  66.4 2.2 fusion.64
  68.6 2.2 fusion.63
  70.9 31.2 %all_gather.25 = bf16[192,768]{0,1:T(8,128)(2,1)S(1)} all-gather(bf16[192,96]{0,1:T(8,128)(2,1)S(1)} %copy.36), channel_id=1, replica_groups=mesh['shard'=4,'ctx'=2,'tp'=4] {'shard','ctx'}, dimensions={1}, use_global_device_ids=true | all-gather | bytes 331776 | tf_op jit(solution)/shard_map/all_gather | solution.py:69
  102.1 4.2 fusion.13
  110.7 1.6 fusion.39
  113.6 41.2 %all-reduce.6.cloned.1.call-done = f32[512,768]{1,0:T(8,128)} async-done(((f32[512,768]{1,0:T(8,128)}), f32[512,768]{1,0:T(8,128)}) %all-reduce.6.cloned.1.call-update) | async-done | bytes 1572880 | tf_op jit(solution)/shard_map/psum | solution.py:103
  154.8 1.7 fusion.59
  157.2 3.3 convolution_add_fusion
  160.5 37.3 %all-gather.5.cloned.1.call-done = bf16[768,768]{0,1:T(8,128)(2,1)} async-done(((bf16[768,96]{0,1:T(8,128)(2,1)}), bf16[768,768]{0,1:T(8,128)(2,1)}) %all-gather.5.cloned.1.call-update) | async-done | bytes 1179664 | tf_op jit(solution)/shard_map/all_gather | solution.py:71
  197.8 4.0 fusion.48
  202.1 1.4 convert_element_type.154
  203.5 39.9 %all-reduce.8.cloned.1.call-done = f32[512,768]{1,0:T(8,128)} async-done(((f32[512,768]{1,0:T(8,128)}), f32[512,768]{1,0:T(8,128)}) %all-reduce.8.cloned.1.call-update) | async-done | bytes 1572880 | tf_op jit(solution)/shard_map/psum | solution.py:111
  243.3 3.6 fusion.9
  249.5 1.6 fusion.57
  251.9 1.3 copy-done.75
  253.2 2.2 convert_reduce_fusion.1
  256.3 2.0 fusion.66
  260.9 40.4 %all-reduce.10.cloned.1.call-done = f32[512,768]{1,0:T(8,128)} async-done(((f32[512,768]{1,0:T(8,128)}), f32[512,768]{1,0:T(8,128)}) %all-reduce.10.cloned.1.call-update) | async-done | bytes 1572880 | tf_op jit(solution)/shard_map/psum | solution.py:128
  301.3 3.3 multiply_reduce_fusion.3
  309.6 2.8 multiply_reduce_fusion.2
  317.9 2.0 fusion.25
  320.4 1.3 copy-done.9
  323.1 2.6 convolution_bitcast_fusion.3
  325.8 1.8 fusion.20
  327.6 1.7 fusion.19
  329.3 1.3 fusion.18
  330.6 4.6 reduce-scatter.11.cloned.1.call-done
  336.3 18.6 %reduce-scatter.13.cloned.1.call-done = f32[1,512,192]{1,2,0:T(8,128)} async-done(((f32[1,1024,192]{1,2,0:T(8,128)}), f32[1,512,192]{1,2,0:T(8,128)}) %reduce-scatter.13.cloned.1.call-update) | async-done | bytes 393232 | tf_op jit(solution)/shard_map/reduce_scatter | solution.py:176
  354.9 1.7 convert_reduce_fusion.3
  357.3 3.4 convolution_bitcast_fusion.1
  360.8 3.1 convolution_bitcast_fusion
  363.9 4.2 copy.39
  368.1 4.7 reshape.271
  373.5 3.5 fusion.49
  378.1 3.8 fusion.47
  383.3 2.6 pad_maximum_fusion.6
  386.0 34.5 %reduce-scatter.21.cloned.1.call-done = f32[96,192]{1,0:T(8,128)} async-done(((f32[768,192]{1,0:T(8,128)}), f32[96,192]{1,0:T(8,128)}) %reduce-scatter.21.cloned.1.call-update) | async-done | bytes 73744
  420.5 1.6 copy.42
  422.2 35.7 %all-reduce = (f32[2,192]{1,0:T(2,128)}, f32[768]{0:T(1024)}, f32[768]{0:T(1024)}, f32[768]{0:T(1024)}, f32[768]{0:T(1024)}, /*index=5*/f32[768]{0:T(1024)}, f32[768]{0:T(1024)}, f32[768]{0:T(1024)}, f32[4]{0:T(128)S(1)}) all-reduce(f32[2,192]{1,0:T(2,128)S(1)} %pad_maximum_fusion.5, ...), channel_id=1, replica_groups=mesh['shard'=4,'ctx'=2,'tp'=4] {'shard','ctx'}, use_global_device_ids=true, to_apply=%region_26.27 | all-reduce | flops 5764 | bytes 46112 | tf_op jit(solution)/shard_map/psum | solution.py:208
  459.7 5.2 all-reduce.12.cloned.1.call-done
  465.0 2.8 add_bitcast_fusion
  467.7 67.9 %reduce-scatter.19.cloned.1.call-done = f32[96,576]{1,0:T(8,128)} async-done(((f32[768,576]{1,0:T(8,128)}), f32[96,576]{1,0:T(8,128)}) %reduce-scatter.19.cloned.1.call-update) | async-done | bytes 221200
  537.5 70.1 %reduce-scatter.15.cloned.1.call-done = f32[96,768]{1,0:T(8,128)} async-done(((f32[768,768]{1,0:T(8,128)}), f32[96,768]{1,0:T(8,128)}) %reduce-scatter.15.cloned.1.call-update) | async-done | bytes 294928 | tf_op jit(solution)/shard_map/reduce_scatter | solution.py:195
  607.6 72.0 %reduce-scatter.17.cloned.1.call-done = f32[768,96]{0,1:T(8,128)} async-done(((f32[768,768]{0,1:T(8,128)}), f32[768,96]{0,1:T(8,128)}) %reduce-scatter.17.cloned.1.call-update) | async-done | bytes 294928 | tf_op jit(solution)/shard_map/reduce_scatter | solution.py:196
  (235 shorter events, 37.4 us)
Async XLA Ops:
  8.0 46.3 %copy-start.15 = (bf16[1,512,768]{2,1,0:T(8,128)(2,1)S(1)}, bf16[1,512,768]{2,1,0:T(8,128)(2,1)}, u32[]{:S(2)}) copy-start(bf16[1,512,768]{2,1,0:T(8,128)(2,1)} %param.16) | copy-start | bytes 2359300
  8.0 146.7 %all-reduce.6.cloned.1.call-start = ((), (), s32[]{:S(2)}) async-start(), calls=%async_computation.6 | async-start | bytes 3145728 | tf_op jit(solution)/shard_map/psum | solution.py:103
  14.1 95.0 %copy-start.63 = (pred[1024]{0:T(1024)(128)(4,1)}, pred[1024]{0:T(1024)(128)(4,1)S(1)}, u32[]{:S(2)}) copy-start(pred[1024]{0:T(1024)(128)(4,1)S(1)} %compare_reduce_fusion) | copy-start | bytes 3076
  14.1 95.0 %copy-start.45 = (s32[1,1,1024]{2,1,0:T(1,128)}, s32[1,1,1024]{2,1,0:T(1,128)S(1)}, u32[]{:S(2)}) copy-start(s32[1,1,1024]{2,1,0:T(1,128)S(1)} %slice.118) | copy-start | bytes 12292
  14.1 95.0 %copy-start.57 = (s32[512]{0:T(512)}, s32[512]{0:T(512)S(1)}, u32[]{:S(2)}) copy-start(s32[512]{0:T(512)S(1)} %iota_add_fusion) | copy-start | bytes 6148
  55.4 8.7 %copy-start.59 = (s32[1,512]{1,0:T(1,128)S(1)}, s32[1,512]{1,0:T(1,128)}, u32[]{:S(2)}) copy-start(s32[1,512]{1,0:T(1,128)} %param.17) | copy-start | bytes 6148
  55.6 13.1 %copy-start.29 = (bf16[1,512,192]{1,2,0:T(8,128)(2,1)}, bf16[1,512,192]{1,2,0:T(8,128)(2,1)S(1)}, u32[]{:S(2)}) copy-start(bf16[1,512,192]{1,2,0:T(8,128)(2,1)S(1)} %fusion.34) | copy-start | bytes 589828
  64.2 45.0 %copy-start.16 = (bf16[2,1,1024,192]{2,3,1,0:T(8,128)(2,1)}, bf16[2,1,1024,192]{2,3,1,0:T(8,128)(2,1)S(1)}, u32[]{:S(2)}) copy-start(bf16[2,1,1024,192]{2,3,1,0:T(8,128)(2,1)S(1)} %all_gather.24) | copy-start | bytes 2359300
  66.4 41.2 %copy-start.51 = (f32[512]{0:T(512)}, f32[512]{0:T(512)S(1)}, u32[]{:S(2)}) copy-start(f32[512]{0:T(512)S(1)} %get-tuple-element.107) | copy-start | bytes 6148
  68.6 40.6 %copy-start.52 = (f32[512]{0:T(512)}, f32[512]{0:T(512)S(1)}, u32[]{:S(2)}) copy-start(f32[512]{0:T(512)S(1)} %get-tuple-element.105) | copy-start | bytes 6148
  68.6 2.2 copy-start.38
  70.8 35.5 %copy-start.53 = (f32[512]{0:T(512)}, f32[512]{0:T(512)S(1)}, u32[]{:S(2)}) copy-start(f32[512]{0:T(512)S(1)} %get-tuple-element.103) | copy-start | bytes 6148
  102.1 4.3 copy-start.22
  106.3 2.8 copy-start.55
  107.6 3.1 copy-start.31
  110.7 44.0 %copy-start.47 = (f32[768]{0:T(1024)S(1)}, f32[768]{0:T(1024)}, u32[]{:S(2)}) copy-start(f32[768]{0:T(1024)} %param.22) | copy-start | bytes 9220
  112.3 44.5 %all-gather.3.cloned.1.call-start = ((), (), s32[]{:S(2)}) async-start(), calls=%async_computation.7 | async-start | bytes 1327104 | tf_op jit(solution)/shard_map/all_gather | solution.py:70
  112.9 84.9 %all-gather.5.cloned.1.call-start = ((), (), s32[]{:S(2)}) async-start(), calls=%async_computation.8 | async-start | bytes 1327104 | tf_op jit(solution)/shard_map/all_gather | solution.py:71
  113.5 129.8 %all-reduce.8.cloned.1.call-start = ((), (), s32[]{:S(2)}) async-start(), calls=%async_computation.9 | async-start | bytes 3145728 | tf_op jit(solution)/shard_map/psum | solution.py:111
  201.8 41.5 %copy-start.14 = (f32[512,768]{1,0:T(8,128)S(1)}, f32[512,768]{1,0:T(8,128)}, u32[]{:S(2)}) copy-start(f32[512,768]{1,0:T(8,128)} %all-reduce.6.cloned.1.call-done) | copy-start | bytes 4718596
  201.8 99.5 %all-reduce.10.cloned.1.call-start = ((), (), s32[]{:S(2)}) async-start(), calls=%async_computation.10 | async-start | bytes 3145728 | tf_op jit(solution)/shard_map/psum | solution.py:128
  249.5 2.4 copy-start.78
  251.1 4.3 copy-start.3
  251.1 2.1 copy-start.75
  251.1 4.3 copy-start.41
  251.9 3.5 copy-start.27
  253.2 3.1 copy-start.74
  258.3 77.0 %reduce-scatter.11.cloned.1.call-start = ((), (), s32[]{:S(2)}) async-start(), calls=%async_computation.11 | async-start | bytes 1179648 | tf_op jit(solution)/shard_map/reduce_scatter | solution.py:175
  305.3 2.7 copy-start.23
  307.5 2.0 copy-start.19
  312.4 2.7 copy-start.12
  315.7 2.2 copy-start.26
  317.6 37.3 %reduce-scatter.13.cloned.1.call-start = ((), (), s32[]{:S(2)}) async-start(), calls=%async_computation.12 | async-start | bytes 1179648 | tf_op jit(solution)/shard_map/reduce_scatter | solution.py:176
  317.9 2.2 copy-start.11
  323.0 97.5 %reduce-scatter.21.cloned.1.call-start = ((), (), s32[]{:S(2)}) async-start(), calls=%async_computation.17 | async-start | bytes 884736
  325.8 139.2 %all-reduce.12.cloned.1.call-start = ((), (), s32[]{:S(2)}) async-start(), calls=%async_computation.13 | async-start | bytes 3145728 | tf_op jit(solution)/shard_map/psum | solution.py:188
  325.8 3.4 copy-start.7
  360.7 174.9 %reduce-scatter.19.cloned.1.call-start = ((), (), s32[]{:S(2)}) async-start(), calls=%async_computation.16 | async-start | bytes 2211840
  372.8 234.8 %reduce-scatter.15.cloned.1.call-start = ((), (), s32[]{:S(2)}) async-start(), calls=%async_computation.14 | async-start | bytes 2654208 | tf_op jit(solution)/shard_map/reduce_scatter | solution.py:195
  377.0 302.6 %reduce-scatter.17.cloned.1.call-start = ((), (), s32[]{:S(2)}) async-start(), calls=%async_computation.15 | async-start | bytes 2654208 | tf_op jit(solution)/shard_map/reduce_scatter | solution.py:196
  382.0 40.2 %copy-start.65 = (f32[192]{0:T(256)S(1)}, f32[192]{0:T(256)}, u32[]{:S(2)}) copy-start(f32[192]{0:T(256)} %get-tuple-element.71) | copy-start | bytes 2308
  382.0 40.2 %copy-start.42 = (f32[768]{0:T(1024)S(1)}, f32[768]{0:T(1024)}, u32[]{:S(2)}) copy-start(f32[768]{0:T(1024)} %get-tuple-element.45) | copy-start | bytes 9220
  382.0 40.2 %copy-start.43 = (f32[768]{0:T(1024)S(1)}, f32[768]{0:T(1024)}, u32[]{:S(2)}) copy-start(f32[768]{0:T(1024)} %get-tuple-element.65) | copy-start | bytes 9220
  382.0 40.2 %copy-start.44 = (f32[768]{0:T(1024)S(1)}, f32[768]{0:T(1024)}, u32[]{:S(2)}) copy-start(f32[768]{0:T(1024)} %get-tuple-element.69) | copy-start | bytes 9220
  382.1 40.2 %copy-start.49 = (f32[768]{0:T(1024)S(1)}, f32[768]{0:T(1024)}, u32[]{:S(2)}) copy-start(f32[768]{0:T(1024)} %get-tuple-element.47) | copy-start | bytes 9220
  382.1 40.2 %copy-start.50 = (f32[768]{0:T(1024)S(1)}, f32[768]{0:T(1024)}, u32[]{:S(2)}) copy-start(f32[768]{0:T(1024)} %get-tuple-element.49) | copy-start | bytes 9220
  382.1 40.2 %copy-start.66 = (f32[768]{0:T(1024)S(1)}, f32[768]{0:T(1024)}, u32[]{:S(2)}) copy-start(f32[768]{0:T(1024)} %get-tuple-element.67) | copy-start | bytes 9220
  382.1 82.9 %copy-start.2 = (f32[512,768]{1,0:T(8,128)S(1)}, f32[512,768]{1,0:T(8,128)}, u32[]{:S(2)}) copy-start(f32[512,768]{1,0:T(8,128)} %copy-done.1) | copy-start | bytes 4718596
  (43 other events, 60.7 us)
Sparse Core Ops, SparseCore 0:
  112.5 42.2 all-reduce.5
  202.0 41.3 all-reduce.7
  258.4 42.8 all-reduce.9
  317.7 17.4 reduce-scatter.10
  337.4 17.4 reduce-scatter.12
  358.1 62.4 reduce-scatter.20
  423.0 41.8 all-reduce.11
  468.8 66.7 reduce-scatter.18
  539.7 67.8 reduce-scatter.14
  611.5 68.0 reduce-scatter.16
Sparse Core Ops, SparseCore 1:
  115.0 40.7 all-gather.2
  157.8 40.0 all-gather.4
where the time goes:
time: 688 us; the launch traced here: 687 us
  waiting for transfers between devices  433 us (63%)
  blocking collectives  119 us (17%)
  matrix products  53 us (8%)
  other arithmetic  34.3 us (5%)
  local copies, waits for them, and re-layouts  29.7 us (4%)
  between operations  17.2 us (2%)
    unnamed x14, waiting for transfers between devices  104 us
    reduce_scatter x1, waiting for transfers between devices, body(): lax.psum_scatter(g_down, ('shard', 'ctx'), scatter_dimension=1, tiled=True)  72 us
    reduce_scatter x1, waiting for transfers between devices, body(): lax.psum_scatter(g_in, ('shard', 'ctx'), scatter_dimension=0, tiled=True)  70.1 us
    psum x1, waiting for transfers between devices, body(): lax.psum(jnp.dot(context, w_out, preferred_element_type=jnp.float32), 'tp')  41.2 us
    psum x1, waiting for transfers between devices, body(): lax.psum(jnp.einsum('nf,df->nd', d_pre, w_in, preferred_element_type=jnp....  40.4 us
    psum x1, waiting for transfers between devices, body(): lax.psum(jnp.dot(act_low, w_down, preferred_element_type=jnp.float32), 'tp')  39.9 us
    all_gather x1, blocking collectives, body(): lax.all_gather(qkv_weight, ('shard', 'ctx'), axis=1, tiled=True)  38.3 us
    all_gather x1, waiting for transfers between devices, body(): lax.all_gather(down_weight, ('shard', 'ctx'), axis=1, tiled=True)  37.3 us
  transfers between devices with their start and end apart: 12, of which 11 were waited for; matrix products, arithmetic and copies ran while one was open for 8% of the time, Pallas kernels for 0%

commit v1 on v0

--- a/solution.py
+++ b/solution.py
@@ -6,6 +6,18 @@
 HEAD_DIM = 64
 norm_eps = 1e-12
 masked_score = -1e30
+
+
+def gather_by_bits(x, axis, dim):
+    ways, here = (lax.axis_size(axis), lax.axis_index(axis))
+    grown, reach = (x, 1)
+    while reach < ways:
+        theirs = lax.ppermute(grown, axis, [(d, d ^ reach) for d in range(ways)])
+        mine_first = jnp.concatenate([grown, theirs], axis=dim)
+        theirs_first = jnp.concatenate([theirs, grown], axis=dim)
+        grown = jnp.where(here & reach == 0, mine_first, theirs_first)
+        reach = 2 * reach
+    return grown
 
 
 def layer_norm(rows, gain, shift):
@@ -66,7 +78,7 @@
     heads_here = cols // HEAD_DIM
     w_qkv, w_out, w_in, w_down = (
         lax.all_gather(qkv_weight, ("shard", "ctx"), axis=1, tiled=True),
-        lax.all_gather(out_weight, ("shard", "ctx"), axis=1, tiled=True),
+        gather_by_bits(out_weight, ("shard", "ctx"), 1),
         lax.all_gather(in_weight, ("shard", "ctx"), axis=0, tiled=True),
         lax.all_gather(down_weight, ("shard", "ctx"), axis=1, tiled=True),
     )

time: 688 us -> 663 us (0.964)
  waiting for transfers between devices: 433 us -> 410 us
    psum x1, waiting for transfers between devices: 40.4 us -> 10.1 us  [body(): lax.psum(jnp.einsum('nf,df->nd', d_pre, w_in, preferred_element_type=jnp....]
    unnamed x165 -> x159, local copies, waits for them, and re-layouts: 27.1 us -> 27.8 us
  transfers between devices with their start and end apart: 12 -> 15, of which waited for: 11 -> 13; matrix products, arithmetic and copies ran while one was open for 8% -> 10% of each run, Pallas kernels for 0% -> 0%
where the time goes in v1:
time: 663 us; the launch traced here: 662 us
  waiting for transfers between devices  410 us (62%)
  blocking collectives  117 us (18%)
  matrix products  50.8 us (8%)
  local copies, waits for them, and re-layouts  30.4 us (5%)
  other arithmetic  29.8 us (4%)
  between operations  17.2 us (3%)
    unnamed x14, waiting for transfers between devices  104 us
    reduce_scatter x1, waiting for transfers between devices, body(): lax.psum_scatter(g_down, ('shard', 'ctx'), scatter_dimension=1, tiled=True)  72 us
    reduce_scatter x1, waiting for transfers between devices, body(): lax.psum_scatter(g_in, ('shard', 'ctx'), scatter_dimension=0, tiled=True)  70.7 us
    psum x1, waiting for transfers between devices, body(): lax.psum(jnp.dot(context, w_out, preferred_element_type=jnp.float32), 'tp')  41.3 us
    psum x1, waiting for transfers between devices, body(): lax.psum(jnp.dot(act_low, w_down, preferred_element_type=jnp.float32), 'tp')  40.1 us
    all_gather x1, waiting for transfers between devices, body(): lax.all_gather(down_weight, ('shard', 'ctx'), axis=1, tiled=True)  38.5 us
    all_gather x1, blocking collectives, body(): lax.all_gather(qkv_weight, ('shard', 'ctx'), axis=1, tiled=True)  37.1 us
    psum x1, blocking collectives, body(): lax.psum((d_qv_bias, d_out_bias, d_gain1, d_shift1, d_in_bias, d_down_bia...  35.8 us
  transfers between devices with their start and end apart: 15, of which 13 were waited for; matrix products, arithmetic and copies ran while one was open for 10% of the time, Pallas kernels for 0%

profile of v1, /device:TPU:0, one launch (start us, length us, event | category | flops | bytes accessed | tf_op | source)
XLA Modules:
  0.0 661.8 jit_solution(7252218407377217774)
XLA Ops:
  8.1 3.0 collective-permute-start
  11.8 4.3 all_gather.21
  18.0 37.1 %all_gather.22 = bf16[3,768,192]{2,0,1:T(4,128)(2,1)S(1)} all-gather(bf16[3,96,192]{2,0,1:T(4,128)(2,1)S(1)} %copy.34), channel_id=1, replica_groups=mesh['shard'=4,'ctx'=2,'tp'=4] {'shard','ctx'}, dimensions={1}, use_global_device_ids=true | all-gather | bytes 995328 | tf_op jit(solution)/shard_map/all_gather | solution.py:80
  56.6 8.5 %all_gather.23 = bf16[2,1,1024,192]{2,3,1,0:T(8,128)(2,1)S(1)} all-gather(bf16[2,1,512,192]{2,3,1,0:T(8,128)(2,1)S(1)} %pad_maximum_fusion.1), channel_id=1, replica_groups=mesh['shard'=4,'ctx'=2,'tp'=4] {'ctx'}, dimensions={2}, use_global_device_ids=true | all-gather | bytes 1179648 | tf_op jit(solution)/shard_map/all_gather | solution.py:91
  68.3 2.3 fusion.13
  72.6 2.7 convolution_convert_fusion.1
  76.7 1.5 collective-permute-start.2
  78.2 2.7 convolution_convert_fusion.2
  81.0 3.4 collective-permute-done.2
  84.4 1.6 fusion.35
  87.4 41.3 %all-reduce.6.cloned.1.call-done = f32[512,768]{1,0:T(8,128)} async-done(((f32[512,768]{1,0:T(8,128)}), f32[512,768]{1,0:T(8,128)}) %all-reduce.6.cloned.1.call-update) | async-done | bytes 1572880 | tf_op jit(solution)/shard_map/psum | solution.py:115
  128.7 1.7 fusion.65
  131.2 2.2 convolution_add_fusion
  133.4 38.5 %all-gather.5.cloned.1.call-done = bf16[768,768]{0,1:T(8,128)(2,1)} async-done(((bf16[768,96]{0,1:T(8,128)(2,1)}), bf16[768,768]{0,1:T(8,128)(2,1)}) %all-gather.5.cloned.1.call-update) | async-done | bytes 1179664 | tf_op jit(solution)/shard_map/all_gather | solution.py:83
  171.8 3.5 fusion.54
  176.7 40.1 %all-reduce.8.cloned.1.call-done = f32[512,768]{1,0:T(8,128)} async-done(((f32[512,768]{1,0:T(8,128)}), f32[512,768]{1,0:T(8,128)}) %all-reduce.8.cloned.1.call-update) | async-done | bytes 1572880 | tf_op jit(solution)/shard_map/psum | solution.py:123
  216.8 3.6 fusion.9
  223.1 1.6 fusion.63
  226.7 2.2 convert_reduce_fusion.1
  229.8 2.0 fusion.72
  231.9 31.6 %all_gather.26 = bf16[192,768]{0,1:T(8,128)(2,1)S(1)} all-gather(bf16[192,96]{0,1:T(8,128)(2,1)} %copy.36), channel_id=1, replica_groups=mesh['shard'=4,'ctx'=2,'tp'=4] {'shard','ctx'}, dimensions={1}, use_global_device_ids=true | all-gather | bytes 331776 | tf_op jit(solution)/shard_map/all_gather | solution.py:128
  264.8 10.1 %all-reduce.10.cloned.1.call-done = f32[512,768]{1,0:T(8,128)} async-done(((f32[512,768]{1,0:T(8,128)}), f32[512,768]{1,0:T(8,128)}) %all-reduce.10.cloned.1.call-update) | async-done | bytes 1572880 | tf_op jit(solution)/shard_map/psum | solution.py:140
  274.9 3.3 multiply_reduce_fusion.3
  283.1 2.8 multiply_reduce_fusion.2
  291.3 2.0 fusion.25
  293.8 1.3 copy-done.9
  296.5 2.6 convolution_bitcast_fusion.3
  299.2 1.8 fusion.20
  300.9 1.7 fusion.19
  302.6 1.4 fusion.18
  304.0 4.9 reduce-scatter.11.cloned.1.call-done
  309.9 18.6 %reduce-scatter.13.cloned.1.call-done = f32[1,512,192]{1,2,0:T(8,128)} async-done(((f32[1,1024,192]{1,2,0:T(8,128)}), f32[1,512,192]{1,2,0:T(8,128)}) %reduce-scatter.13.cloned.1.call-update) | async-done | bytes 393232 | tf_op jit(solution)/shard_map/reduce_scatter | solution.py:188
  328.5 1.7 convert_reduce_fusion.3
  330.9 3.4 convolution_bitcast_fusion.1
  334.4 3.2 convolution_bitcast_fusion
  337.5 4.3 copy.39
  341.8 4.7 reshape.271
  347.2 3.5 fusion.55
  351.9 3.9 fusion.53
  357.0 2.6 pad_maximum_fusion.6
  359.7 34.5 %reduce-scatter.21.cloned.1.call-done = f32[96,192]{1,0:T(8,128)} async-done(((f32[768,192]{1,0:T(8,128)}), f32[96,192]{1,0:T(8,128)}) %reduce-scatter.21.cloned.1.call-update) | async-done | bytes 73744
  394.2 1.6 copy.42
  395.9 35.8 %all-reduce = (f32[2,192]{1,0:T(2,128)}, f32[768]{0:T(1024)}, f32[768]{0:T(1024)}, f32[768]{0:T(1024)}, f32[768]{0:T(1024)}, /*index=5*/f32[768]{0:T(1024)}, f32[768]{0:T(1024)}, f32[768]{0:T(1024)}, f32[4]{0:T(128)S(1)}) all-reduce(f32[2,192]{1,0:T(2,128)S(1)} %pad_maximum_fusion.5, ...), channel_id=1, replica_groups=mesh['shard'=4,'ctx'=2,'tp'=4] {'shard','ctx'}, use_global_device_ids=true, to_apply=%region_26.27 | all-reduce | flops 5764 | bytes 46112 | tf_op jit(solution)/shard_map/psum | solution.py:220
  433.4 5.7 all-reduce.12.cloned.1.call-done
  439.2 2.8 add_bitcast_fusion
  441.9 67.9 %reduce-scatter.19.cloned.1.call-done = f32[96,576]{1,0:T(8,128)} async-done(((f32[768,576]{1,0:T(8,128)}), f32[96,576]{1,0:T(8,128)}) %reduce-scatter.19.cloned.1.call-update) | async-done | bytes 221200
  511.7 70.7 %reduce-scatter.15.cloned.1.call-done = f32[96,768]{1,0:T(8,128)} async-done(((f32[768,768]{1,0:T(8,128)}), f32[96,768]{1,0:T(8,128)}) %reduce-scatter.15.cloned.1.call-update) | async-done | bytes 294928 | tf_op jit(solution)/shard_map/reduce_scatter | solution.py:207
  582.4 72.0 %reduce-scatter.17.cloned.1.call-done = f32[768,96]{0,1:T(8,128)} async-done(((f32[768,768]{0,1:T(8,128)}), f32[768,96]{0,1:T(8,128)}) %reduce-scatter.17.cloned.1.call-update) | async-done | bytes 294928 | tf_op jit(solution)/shard_map/reduce_scatter | solution.py:208
  (237 shorter events, 40.7 us)
Async XLA Ops:
  8.0 47.1 %copy-start.15 = (bf16[1,512,768]{2,1,0:T(8,128)(2,1)S(1)}, bf16[1,512,768]{2,1,0:T(8,128)(2,1)}, u32[]{:S(2)}) copy-start(bf16[1,512,768]{2,1,0:T(8,128)(2,1)} %param.16) | copy-start | bytes 2359300
  8.0 120.7 %all-reduce.6.cloned.1.call-start = ((), (), s32[]{:S(2)}) async-start(), calls=%async_computation.6 | async-start | bytes 3145728 | tf_op jit(solution)/shard_map/psum | solution.py:115
  8.1 63.7 %collective-permute-start = (bf16[192,96]{1,0:T(8,128)(2,1)}, bf16[192,96]{1,0:T(8,128)(2,1)S(1)}, u32[]{:S(2)}, u32[]{:S(2)}) collective-permute-start(bf16[192,96]{1,0:T(8,128)(2,1)} %param.21), channel_id=1, source_target_pairs={{0,4},{4,0},{8,12},{12,8},{16,20},{20,16},{24,28},{28,24},{1,5},{5... | collective-permute-start | bytes 110600 | tf_op jit(solution)/shard_map/ppermute | solution.py:15
  16.1 62.1 %copy-start.59 = (pred[1024]{0:T(1024)(128)(4,1)}, pred[1024]{0:T(1024)(128)(4,1)S(1)}, u32[]{:S(2)}) copy-start(pred[1024]{0:T(1024)(128)(4,1)S(1)} %compare_reduce_fusion) | copy-start | bytes 3076
  16.1 62.0 %copy-start.46 = (s32[1,1,1024]{2,1,0:T(1,128)}, s32[1,1,1024]{2,1,0:T(1,128)S(1)}, u32[]{:S(2)}) copy-start(s32[1,1,1024]{2,1,0:T(1,128)S(1)} %slice.118) | copy-start | bytes 12292
  16.2 62.0 %copy-start.52 = (s32[512]{0:T(512)}, s32[512]{0:T(512)S(1)}, u32[]{:S(2)}) copy-start(s32[512]{0:T(512)S(1)} %iota_add_fusion) | copy-start | bytes 6148
  56.3 8.7 %copy-start.54 = (s32[1,512]{1,0:T(1,128)S(1)}, s32[1,512]{1,0:T(1,128)}, u32[]{:S(2)}) copy-start(s32[1,512]{1,0:T(1,128)} %param.17) | copy-start | bytes 6148
  56.4 10.6 %copy-start.29 = (bf16[1,512,192]{1,2,0:T(8,128)(2,1)}, bf16[1,512,192]{1,2,0:T(8,128)(2,1)S(1)}, u32[]{:S(2)}) copy-start(bf16[1,512,192]{1,2,0:T(8,128)(2,1)S(1)} %fusion.34) | copy-start | bytes 589828
  65.0 13.2 %copy-start.16 = (bf16[2,1,1024,192]{2,3,1,0:T(8,128)(2,1)}, bf16[2,1,1024,192]{2,3,1,0:T(8,128)(2,1)S(1)}, u32[]{:S(2)}) copy-start(bf16[2,1,1024,192]{2,3,1,0:T(8,128)(2,1)S(1)} %all_gather.23) | copy-start | bytes 2359300
  67.9 2.6 copy-start.22
  71.7 12.7 %copy-start.33 = (bf16[512,64]{0,1:T(8,128)(2,1)}, bf16[512,64]{0,1:T(8,128)(2,1)S(1)}, u32[]{:S(2)}) copy-start(bf16[512,64]{0,1:T(8,128)(2,1)S(1)} %convolution_convert_fusion.3) | copy-start | bytes 196612
  71.9 4.7 collective-permute-start.1
  75.3 9.1 %copy-start.35 = (bf16[512,64]{0,1:T(8,128)(2,1)}, bf16[512,64]{0,1:T(8,128)(2,1)S(1)}, u32[]{:S(2)}) copy-start(bf16[512,64]{0,1:T(8,128)(2,1)S(1)} %convolution_convert_fusion.1) | copy-start | bytes 196612
  76.7 7.7 %collective-permute-start.2 = (bf16[192,384]{1,0:T(8,128)(2,1)S(1)}, bf16[192,384]{1,0:T(8,128)(2,1)S(1)}, u32[]{:S(2)}, u32[]{:S(2)}) collective-permute-start(bf16[192,384]{1,0:T(8,128)(2,1)S(1)} %maximum_select_fusion.2), channel_id=1, source_target_pairs={{0,16},{4,20},{8,24},{12,28},{16,0},{20,4},{24,8},{28,12},{1,17},{... | collective-permute-start | bytes 442376 | tf_op jit(solution)/shard_map/ppermute | solution.py:15
  80.9 5.1 copy-start.37
  80.9 47.8 %copy-start.48 = (f32[768]{0:T(1024)S(1)}, f32[768]{0:T(1024)}, u32[]{:S(2)}) copy-start(f32[768]{0:T(1024)} %param.22) | copy-start | bytes 9220
  86.0 44.8 %all-gather.3.cloned.1.call-start = ((), (), s32[]{:S(2)}) async-start(), calls=%async_computation.7 | async-start | bytes 1327104 | tf_op jit(solution)/shard_map/all_gather | solution.py:82
  86.6 85.2 %all-gather.5.cloned.1.call-start = ((), (), s32[]{:S(2)}) async-start(), calls=%async_computation.8 | async-start | bytes 1327104 | tf_op jit(solution)/shard_map/all_gather | solution.py:83
  87.2 129.7 %all-reduce.8.cloned.1.call-start = ((), (), s32[]{:S(2)}) async-start(), calls=%async_computation.9 | async-start | bytes 3145728 | tf_op jit(solution)/shard_map/psum | solution.py:123
  133.3 38.5 %copy-start.74 = (f32[512,768]{1,0:T(8,128)}, f32[512,768]{1,0:T(8,128)S(1)}, u32[]{:S(2)}) copy-start(f32[512,768]{1,0:T(8,128)S(1)} %convolution_add_fusion) | copy-start | bytes 4718596
  175.3 41.5 %copy-start.14 = (f32[512,768]{1,0:T(8,128)S(1)}, f32[512,768]{1,0:T(8,128)}, u32[]{:S(2)}) copy-start(f32[512,768]{1,0:T(8,128)} %all-reduce.6.cloned.1.call-done) | copy-start | bytes 4718596
  175.3 41.5 %copy-start.56 = (f32[768]{0:T(1024)S(1)}, f32[768]{0:T(1024)}, u32[]{:S(2)}) copy-start(f32[768]{0:T(1024)} %param.28) | copy-start | bytes 9220
  175.3 99.5 %all-reduce.10.cloned.1.call-start = ((), (), s32[]{:S(2)}) async-start(), calls=%async_computation.10 | async-start | bytes 3145728 | tf_op jit(solution)/shard_map/psum | solution.py:140
  223.1 2.4 copy-start.75
  224.6 4.2 copy-start.3
  224.6 2.1 copy-start.71
  224.6 4.2 copy-start.42
  225.5 3.4 copy-start.27
  226.7 3.1 copy-start.70
  231.8 77.1 %reduce-scatter.11.cloned.1.call-start = ((), (), s32[]{:S(2)}) async-start(), calls=%async_computation.11 | async-start | bytes 1179648 | tf_op jit(solution)/shard_map/reduce_scatter | solution.py:187
  278.8 2.7 copy-start.23
  285.9 2.7 copy-start.12
  291.2 37.3 %reduce-scatter.13.cloned.1.call-start = ((), (), s32[]{:S(2)}) async-start(), calls=%async_computation.12 | async-start | bytes 1179648 | tf_op jit(solution)/shard_map/reduce_scatter | solution.py:188
  291.3 2.2 copy-start.11
  296.4 97.8 %reduce-scatter.21.cloned.1.call-start = ((), (), s32[]{:S(2)}) async-start(), calls=%async_computation.17 | async-start | bytes 884736
  299.1 140.1 %all-reduce.12.cloned.1.call-start = ((), (), s32[]{:S(2)}) async-start(), calls=%async_computation.13 | async-start | bytes 3145728 | tf_op jit(solution)/shard_map/psum | solution.py:200
  299.2 3.4 copy-start.7
  334.3 175.5 %reduce-scatter.19.cloned.1.call-start = ((), (), s32[]{:S(2)}) async-start(), calls=%async_computation.16 | async-start | bytes 2211840
  346.5 235.9 %reduce-scatter.15.cloned.1.call-start = ((), (), s32[]{:S(2)}) async-start(), calls=%async_computation.14 | async-start | bytes 2654208 | tf_op jit(solution)/shard_map/reduce_scatter | solution.py:207
  350.7 303.7 %reduce-scatter.17.cloned.1.call-start = ((), (), s32[]{:S(2)}) async-start(), calls=%async_computation.15 | async-start | bytes 2654208 | tf_op jit(solution)/shard_map/reduce_scatter | solution.py:208
  355.7 40.1 %copy-start.61 = (f32[192]{0:T(256)S(1)}, f32[192]{0:T(256)}, u32[]{:S(2)}) copy-start(f32[192]{0:T(256)} %get-tuple-element.71) | copy-start | bytes 2308
  355.8 40.1 %copy-start.43 = (f32[768]{0:T(1024)S(1)}, f32[768]{0:T(1024)}, u32[]{:S(2)}) copy-start(f32[768]{0:T(1024)} %get-tuple-element.45) | copy-start | bytes 9220
  355.8 40.1 %copy-start.44 = (f32[768]{0:T(1024)S(1)}, f32[768]{0:T(1024)}, u32[]{:S(2)}) copy-start(f32[768]{0:T(1024)} %get-tuple-element.65) | copy-start | bytes 9220
  355.8 40.1 %copy-start.45 = (f32[768]{0:T(1024)S(1)}, f32[768]{0:T(1024)}, u32[]{:S(2)}) copy-start(f32[768]{0:T(1024)} %get-tuple-element.69) | copy-start | bytes 9220
  355.8 40.1 %copy-start.50 = (f32[768]{0:T(1024)S(1)}, f32[768]{0:T(1024)}, u32[]{:S(2)}) copy-start(f32[768]{0:T(1024)} %get-tuple-element.47) | copy-start | bytes 9220
  355.8 40.1 %copy-start.51 = (f32[768]{0:T(1024)S(1)}, f32[768]{0:T(1024)}, u32[]{:S(2)}) copy-start(f32[768]{0:T(1024)} %get-tuple-element.49) | copy-start | bytes 9220
  355.8 40.1 %copy-start.62 = (f32[768]{0:T(1024)S(1)}, f32[768]{0:T(1024)}, u32[]{:S(2)}) copy-start(f32[768]{0:T(1024)} %get-tuple-element.67) | copy-start | bytes 9220
  355.8 83.3 %copy-start.2 = (f32[512,768]{1,0:T(8,128)S(1)}, f32[512,768]{1,0:T(8,128)}, u32[]{:S(2)}) copy-start(f32[512,768]{1,0:T(8,128)} %copy-done.1) | copy-start | bytes 4718596
  (43 other events, 61.1 us)
Sparse Core Ops, SparseCore 0:
  86.1 42.5 all-reduce.5
  175.5 41.3 all-reduce.7
  231.9 42.8 all-reduce.9
  291.3 17.4 reduce-scatter.10
  311.0 17.4 reduce-scatter.12
  331.7 62.4 reduce-scatter.20
  397.2 41.8 all-reduce.11
  443.0 66.7 reduce-scatter.18
  513.9 68.4 reduce-scatter.14
  586.3 68.0 reduce-scatter.16
Sparse Core Ops, SparseCore 1:
  88.7 41.0 all-gather.2
  131.8 40.0 all-gather.4
